TPU v7x, 32 devices: a whole 2x2x4 slice. The times are simulated.
32 devices in a mesh: ckpt: 2 (over y), row: 16 (over z, x, core).
Axes of the slice: x: 2, y: 2, z: 4, core: 2. Of those that a mesh axis runs over, the one named last changes fastest.
Arguments:
- activations: bfloat16 [4096, 4096], P(('ckpt', 'row')), parts along dimension 0, may hold values from -6 to 6
- gate_pre: bfloat16 [4096, 7168], P(('ckpt', 'row')), parts along dimension 0, may hold values from -8 to 8
- out_grad: bfloat16 [4096, 4096], P(('ckpt', 'row')), parts along dimension 0, may hold values from -6 to 6
- down_weight: bfloat16 [14336, 4096], P(('ckpt', 'row')), parts along dimension 0, may hold values from -0.09375 to 0.09375
- proj_in: bfloat16 [4096, 64], replicated, may hold values from -0.09375 to 0.09375
- proj_out: bfloat16 [7168, 64], replicated, may hold values from -0.0625 to 0.0625
- stored: bfloat16 [24576, 4096], P(('ckpt', 'row')), parts along dimension 0, may hold values from -0.09375 to 0.09375
- visible: int32 [16], replicated, may hold values from 1 to 12288, as said below
Outputs:
- scores: float32 [32, 12288], P('ckpt', 'row'), parts along dimension 0
There are 2 independent parts, one for each index of `ckpt`. A program takes and returns all parts, laid end to end along the dimension named above; an argument that names none is the same for every part. Nothing has to cross between parts.
Inputs may be any that keep to these rules, and one draw needn't show every extreme that they name: `visible`: some query example sees all 12288 stored examples and some sees exactly one.
All inputs are finite; a program needn't handle non-finite values.
Results may differ from a plain program's by a relative error of at most 0.0064.
Values may be sent and summed in bfloat16 or wider, within the bound.
No kernel may reach another device: no remote copies, remote signals or barrier semaphores. Data moves between devices by JAX's collectives and lax.ppermute only.
A program may use at most 128 MiB of HBM per device.

v0:
```python
import jax
import jax.numpy as jnp
from jax import lax
from jax.sharding import PartitionSpec as P

SEQ_LEN = 128


def partner(value, axis, bit):
    return lax.ppermute(value, axis, [(i, i ^ 1 << bit) for i in range(lax.axis_size(axis))])


def collect(pieces, position, bit_list, sender):
    for bit_level in bit_list:
        partner_rows = sender(pieces, bit_level)
        upper_half = position >> bit_level & 1 == 1
        pieces = jnp.where(
            upper_half,
            jnp.concatenate([partner_rows, pieces], axis=0),
            jnp.concatenate([pieces, partner_rows], axis=0),
        )
    return pieces


def xor_order(slot_data, lane_id, lane_bits):
    lane_total = 1 << lane_bits
    for bit_level in range(lane_bits):
        shaped = slot_data.reshape(
            (lane_total >> bit_level + 1, 2, 1 << bit_level) + slot_data.shape[1:]
        )
        flipped = shaped[:, ::-1].reshape(slot_data.shape)
        slot_data = jnp.where(lane_id >> bit_level & 1 == 1, flipped, slot_data)
    return slot_data


def lane_exchange(slot_data, lane_id, lane_bits):
    lane_total = 1 << lane_bits
    slot_data = xor_order(slot_data, lane_id, lane_bits)
    for bit_level in range(lane_bits):
        shaped = slot_data.reshape(
            (lane_total >> bit_level + 1, 2, 1 << bit_level) + slot_data.shape[1:]
        )
        arrived = partner(shaped[:, 1], "row", bit_level)
        slot_data = jnp.concatenate([shaped[:, :1], arrived[:, None]], axis=1).reshape(
            slot_data.shape
        )
    return xor_order(slot_data, lane_id, lane_bits)


def shards(activations, gate_pre, out_grad, down_weight, proj_in, proj_out, stored, visible):
    devices = lax.axis_size("row")
    position = lax.axis_index("row")
    total_bits = devices.bit_length() - 1
    lane_bits = 3
    lane_total = 1 << lane_bits
    lane_id = position % lane_total
    tokens_dev = activations.shape[0]
    hidden_total = gate_pre.shape[1]
    rows_piece = down_weight.shape[0]
    groups = hidden_total // (rows_piece * lane_total)
    rank_size = proj_in.shape[1]
    weights_lane = collect(
        down_weight,
        position,
        range(lane_bits, total_bits),
        lambda pieces, bit_level: partner(pieces, "row", bit_level),
    )
    grad_group = collect(
        out_grad,
        position,
        range(0, lane_bits),
        lambda pieces, bit_level: partner(pieces, "row", bit_level),
    )
    hidden_block = lax.dot_general(
        grad_group, weights_lane, (((1,), (1,)), ((), ())), preferred_element_type=jnp.float32
    ).astype(jnp.bfloat16)
    received = lane_exchange(
        hidden_block.reshape(lane_total, tokens_dev, groups * rows_piece), lane_id, lane_bits
    )
    full_grad = (
        received.reshape(lane_total, tokens_dev, groups, rows_piece)
        .transpose(1, 2, 0, 3)
        .reshape(tokens_dev, hidden_total)
    )
    up_grad = (
        lax.optimization_barrier(full_grad).astype(jnp.float32)
        * jax.nn.silu(gate_pre.astype(jnp.float32))
    ).astype(jnp.bfloat16)
    out_proj = jnp.dot(up_grad, proj_out, preferred_element_type=jnp.float32).astype(jnp.bfloat16)
    in_proj = jnp.dot(activations, proj_in, preferred_element_type=jnp.float32).astype(jnp.bfloat16)
    examples_dev = tokens_dev // SEQ_LEN
    in_split = in_proj.astype(jnp.float32).reshape(examples_dev, SEQ_LEN, rank_size)
    out_split = out_proj.astype(jnp.float32).reshape(examples_dev, SEQ_LEN, rank_size)
    raw_feature = jnp.einsum(
        "esa,esb->eab", in_split, out_split, preferred_element_type=jnp.float32
    ).reshape(examples_dev, rank_size * rank_size)
    scale = lax.rsqrt(jnp.mean(raw_feature * raw_feature, axis=1, keepdims=True) + 1e-06)
    queries = (raw_feature * scale).astype(jnp.bfloat16)
    stored_rows = stored.shape[0]
    column = position * stored_rows + jnp.arange(stored_rows, dtype=jnp.int32)
    products = lax.dot_general(
        lax.all_gather(queries, "row", axis=0, tiled=True),
        stored,
        (((1,), (1,)), ((), ())),
        preferred_element_type=jnp.float32,
    )
    return jnp.where(column[None, :] < visible[:, None], products, jnp.float32(0.0))


def solution(mesh):
    return jax.shard_map(
        shards,
        mesh=mesh,
        in_specs=(
            P(("ckpt", "row"), None),
            P(("ckpt", "row"), None),
            P(("ckpt", "row"), None),
            P(("ckpt", "row"), None),
            P(),
            P(),
            P(("ckpt", "row"), None),
            P(),
        ),
        out_specs=P("ckpt", "row"),
        check_vma=False,
    )
```

profile of v0, /device:TPU:0, one launch (start us, length us, event | category | flops | bytes accessed | tf_op | source)
XLA Modules:
  0.0 381.6 jit_solution(10606979016936965666)
XLA Ops:
  0.0 0.0 copy-start
  0.0 0.5 collective-permute-start
  0.5 2.6 collective-permute-done
  3.1 3.1 maximum_select_fusion.5
  6.2 2.9 collective-permute-start.1
  9.2 46.0 %collective-permute-done.1 = bf16[256,4096]{1,0:T(8,128)(2,1)} collective-permute-done((bf16[256,4096]{1,0:T(8,128)(2,1)S(1)}, bf16[256,4096]{1,0:T(8,128)(2,1)}, u32[]{:S(2)}, u32[]{:S(2)}) %collective-permute-start.1) | collective-permute-done | bytes 2097184 | tf_op jit(solution)/shard_map/ppermute | solution.py:10
  55.2 4.7 %maximum_select_fusion.4 = bf16[512,4096]{1,0:T(8,128)(2,1)} fusion(bf16[256,4096]{1,0:T(8,128)(2,1)S(1)} %maximum_select_fusion.5, bf16[256,4096]{1,0:T(8,128)(2,1)} %collective-permute-done.1, pred[]{:T(512)S(6)} %eq.30), kind=kLoop, calls=%fused_computation.17 | loop fusion | flops 18874368 | bytes 8388609 | tf_op jit(solution)/shard_map/jit(_where)/select_n | solution.py:17
  59.9 1.8 collective-permute-start.2
  61.8 2.6 collective-permute-start.3
  64.4 165.7 %collective-permute-done.3 = bf16[448,4096]{1,0:T(8,128)(2,1)} collective-permute-done((bf16[448,4096]{1,0:T(8,128)(2,1)}, bf16[448,4096]{1,0:T(8,128)(2,1)}, u32[]{:S(2)}, u32[]{:S(2)}) %collective-permute-start.3) | collective-permute-done | bytes 3670048 | tf_op jit(solution)/shard_map/ppermute | solution.py:10
  230.0 1.0 collective-permute-done.2
  231.0 14.4 %fusion.20 = bf16[1024,896]{1,0:T(8,128)(2,1)S(1)} fusion(bf16[448,4096]{1,0:T(8,128)(2,1)} %param.11, bf16[448,4096]{1,0:T(8,128)(2,1)} %collective-permute-done.3, pred[]{:T(512)S(6)} %eq.32, bf16[512,4096]{1,0:T(8,128)(2,1)} %maximum_select_fusion.4, bf16[512,4096]{1,0:T(8,128)(2,1)} %collective-permute-done.2, pred[]{:T(512)S(6)} %eq.29), kind=kOutput, calls=%fused_computation.35 | convolution fusion | flops 7587889152 | bytes 17563650 | tf_op jit(solution)/shard_map/dot_general | solution.py:74
  245.5 1.5 rev.18
  246.9 3.6 copy.27
  250.5 2.4 copy.28
  252.9 2.9 broadcast_select_fusion
  255.9 2.9 rev.19
  258.8 2.4 copy.30
  261.2 3.0 select_select_fusion.2
  264.2 2.9 rev.20
  267.1 3.6 copy.32
  270.7 3.6 copy.31
  274.3 0.8 select_select_fusion.1
  275.1 1.1 fusion.36
  276.2 0.0 collective-permute-start.4
  276.2 0.6 copy.33
  276.8 2.2 collective-permute-done.4
  279.0 1.6 copy.34
  280.6 0.2 fusion.28
  280.8 3.5 collective-permute-start.5
  284.3 20.7 %collective-permute-done.5 = bf16[2,2,128,896]{2,3,1,0:T(8,128)(2,1)S(1)} collective-permute-done((bf16[2,2,128,896]{2,3,1,0:T(8,128)(2,1)S(1)}, bf16[2,2,128,896]{2,3,1,0:T(8,128)(2,1)S(1)}, u32[]{:S(2)}, u32[]{:S(2)}) %collective-permute-start.5) | collective-permute-done | bytes 917536 | tf_op jit(solution)/shard_map/ppermute | solution.py:10
  304.9 0.2 pad_maximum_fusion
  305.1 1.1 fusion.35
  306.2 0.0 copy-start.1
  306.2 0.0 copy-start.4
  306.2 3.1 collective-permute-start.6
  309.3 3.9 %copy.37 = bf16[128,7168]{0,1:T(8,128)(2,1)} copy(bf16[128,7168]{1,0:T(8,128)(2,1)} %param.9) | data formatting | bytes 3670016 | tf_op args[1]
  313.2 0.0 copy-done
  313.2 0.0 copy-done.4
  313.2 0.5 convolution_convert_fusion
  313.7 15.9 %collective-permute-done.6 = bf16[1,4,128,896]{2,3,1,0:T(8,128)(2,1)S(1)} collective-permute-done((bf16[1,4,128,896]{2,3,1,0:T(8,128)(2,1)}, bf16[1,4,128,896]{2,3,1,0:T(8,128)(2,1)S(1)}, u32[]{:S(2)}, u32[]{:S(2)}) %collective-permute-start.6) | collective-permute-done | bytes 917536 | tf_op jit(solution)/shard_map/ppermute | solution.py:10
  329.7 0.0 copy-start.2
  329.7 0.0 copy-done.1
  329.7 1.6 pad_maximum_fusion.1
  331.3 0.0 copy-done.2
  331.3 1.6 rev.21
  332.9 2.9 maximum_select_fusion.6
  335.9 2.9 rev.22
  338.7 2.9 select_select_fusion
  341.7 2.9 rev.23
  344.6 1.8 select_bitcast_fusion
  346.5 0.0 copy-start.3
  346.5 1.4 copy.36
  347.8 0.8 copy-done.3
  348.6 0.0 copy-start.5
  348.6 4.0 %multiply_reduce_fusion = (f32[]{:T(128)}, f32[64,64]{1,0:T(8,128)S(1)}) fusion(bf16[128,64]{0,1:T(8,128)(2,1)S(1)} %convolution_convert_fusion, bf16[7168,64]{0,1:T(8,128)(2,1)} %param.13, bf16[128,7168]{0,1:T(8,128)(2,1)S(1)} %copy-done.3, bf16[128,7168]{0,1:T(8,128)(2,1)} %bitcast.65), kind=kOutput, calls=%fused_computation.49 | convolution fusion | flops 125845504 | bytes 4620292 | tf_op jit(solution)/shard_map/esa,esb->eab/dot_general | solution.py:94
  353.3 0.1 reshape.191
  353.4 23.0 %all-gather = bf16[16,1,4096]{2,1,0:T(2,128)(2,1)S(1)} all-gather(bf16[1,1,4096]{2,1,0:T(2,128)(2,1)S(1)} %reshape.191), channel_id=1, replica_groups=mesh['ckpt'=2,'row'=16] {'row'}, dimensions={0}, use_global_device_ids=true | all-gather | bytes 139264 | tf_op jit(solution)/shard_map/all_gather | solution.py:102
  376.4 0.0 copy-done.5
  376.4 5.2 %convolution_select_fusion = f32[16,768]{1,0:T(8,128)} fusion(bf16[768,4096]{1,0:T(8,128)(2,1)} %param.14, bf16[16,1,4096]{2,1,0:T(2,128)(2,1)S(1)} %all-gather, s32[768]{0:T(1024)S(1)} %iota_add_fusion, s32[16]{0:T(128)S(1)} %copy-done.5), kind=kOutput, calls=%fused_computation.36 | convolution fusion | flops 100687872 | bytes 6474816 | tf_op jit(solution)/shard_map/dot_general | solution.py:101
  (2 shorter events, 0.0 us)
Async XLA Ops:
  0.0 313.2 %copy-start = (bf16[128,4096]{1,0:T(8,128)(2,1)S(1)}, bf16[128,4096]{1,0:T(8,128)(2,1)}, u32[]{:S(2)}) copy-start(bf16[128,4096]{1,0:T(8,128)(2,1)} %param.8) | copy-start | bytes 3145732
  0.0 3.1 collective-permute-start
  6.2 49.0 %collective-permute-start.1 = (bf16[256,4096]{1,0:T(8,128)(2,1)S(1)}, bf16[256,4096]{1,0:T(8,128)(2,1)}, u32[]{:S(2)}, u32[]{:S(2)}) collective-permute-start(bf16[256,4096]{1,0:T(8,128)(2,1)S(1)} %maximum_select_fusion.5), channel_id=1, source_target_pairs={{0,2},{1,3},{2,0},{3,1},{4,6},{5,7},{6,4},{7,5},{8,10},{9,11},{10,... | collective-permute-start | bytes 6291464 | tf_op jit(solution)/shard_map/ppermute | solution.py:10
  59.9 171.1 %collective-permute-start.2 = (bf16[512,4096]{1,0:T(8,128)(2,1)}, bf16[512,4096]{1,0:T(8,128)(2,1)}, u32[]{:S(2)}, u32[]{:S(2)}) collective-permute-start(bf16[512,4096]{1,0:T(8,128)(2,1)} %maximum_select_fusion.4), channel_id=1, source_target_pairs={{0,4},{1,5},{2,6},{3,7},{4,0},{5,1},{6,2},{7,3},{8,12},{9,13},{10,... | collective-permute-start | bytes 12582920 | tf_op jit(solution)/shard_map/ppermute | solution.py:10
  61.8 168.3 %collective-permute-start.3 = (bf16[448,4096]{1,0:T(8,128)(2,1)}, bf16[448,4096]{1,0:T(8,128)(2,1)}, u32[]{:S(2)}, u32[]{:S(2)}) collective-permute-start(bf16[448,4096]{1,0:T(8,128)(2,1)} %param.11), channel_id=1, source_target_pairs={{0,8},{1,9},{2,10},{3,11},{4,12},{5,13},{6,14},{7,15},{8,0},{9,1},... | collective-permute-start | bytes 11010056 | tf_op jit(solution)/shard_map/ppermute | solution.py:10
  276.2 2.8 collective-permute-start.4
  280.8 24.2 %collective-permute-start.5 = (bf16[2,2,128,896]{2,3,1,0:T(8,128)(2,1)S(1)}, bf16[2,2,128,896]{2,3,1,0:T(8,128)(2,1)S(1)}, u32[]{:S(2)}, u32[]{:S(2)}) collective-permute-start(bf16[2,2,128,896]{2,3,1,0:T(8,128)(2,1)S(1)} %get-tuple-element.8), channel_id=1, source_target_pairs={{0,2},{1,3},{2,0},{3,1},{4,6},{5,7},{6,4},{7,5},{8,10},{9,11},{10,... | collective-permute-start | bytes 2752520 | tf_op jit(solution)/shard_map/ppermute | solution.py:10
  306.2 23.5 %copy-start.1 = (bf16[1,1,4,128,896]{3,4,2,1,0:T(8,128)(2,1)}, bf16[1,1,4,128,896]{3,4,2,1,0:T(8,128)(2,1)S(1)}, u32[]{:S(2)}) copy-start(bf16[1,1,4,128,896]{3,4,2,1,0:T(8,128)(2,1)S(1)} %get-tuple-element.5) | copy-start | bytes 2752516
  306.2 7.1 %copy-start.4 = (bf16[4096,64]{0,1:T(8,128)(2,1)S(1)}, bf16[4096,64]{0,1:T(8,128)(2,1)}, u32[]{:S(2)}) copy-start(bf16[4096,64]{0,1:T(8,128)(2,1)} %param.12) | copy-start | bytes 1572868
  306.2 23.5 %collective-permute-start.6 = (bf16[1,4,128,896]{2,3,1,0:T(8,128)(2,1)}, bf16[1,4,128,896]{2,3,1,0:T(8,128)(2,1)S(1)}, u32[]{:S(2)}, u32[]{:S(2)}) collective-permute-start(bf16[1,4,128,896]{2,3,1,0:T(8,128)(2,1)} %get-tuple-element.6), channel_id=1, source_target_pairs={{0,4},{1,5},{2,6},{3,7},{4,0},{5,1},{6,2},{7,3},{8,12},{9,13},{10,... | collective-permute-start | bytes 2752520 | tf_op jit(solution)/shard_map/ppermute | solution.py:10
  329.7 1.6 copy-start.2
  346.5 2.2 copy-start.3
  348.6 27.8 %copy-start.5 = (s32[16]{0:T(128)S(1)}, s32[16]{0:T(128)}, u32[]{:S(2)}) copy-start(s32[16]{0:T(128)} %param.15) | copy-start | bytes 196
where the time goes:
time: 382 us
  waiting for transfers between devices  254 us (66%)
  local copies, waits for them, and re-layouts  40.9 us (11%)
  other arithmetic  24.3 us (6%)
  matrix products  24 us (6%)
  blocking collectives  23 us (6%)
  starting transfers between devices  14.5 us (4%)
    ppermute x7, waiting for transfers between devices, partner(): lax.ppermute(value, axis, [(i, i ^ 1 << bit) for i in range(lax.axis_size...  254 us
    all_gather x1, blocking collectives, shards(): lax.all_gather(queries, 'row', axis=0, tiled=True)  23 us
    rev x7, local copies, waits for them, and re-layouts, xor_order(): flipped = shaped[:, ::-1].reshape(slot_data.shape)  18.3 us
    ppermute x7, starting transfers between devices, partner(): lax.ppermute(value, axis, [(i, i ^ 1 << bit) for i in range(lax.axis_size...  14.5 us
    dot_general x1, matrix products, shards(): lax.dot_general(grad_group, weights_lane, (((1,), (1,)), ((), ())), prefe...  14.4 us
    select_n x5, other arithmetic, xor_order(): slot_data = jnp.where(lane_id >> bit_level & 1 == 1, flipped, slot_data)  12.6 us
    select_n x2, other arithmetic, collect(): jnp.where(upper_half, jnp.concatenate([partner_rows, pieces], axis=0), jn...  7.89 us
  transfers between devices with their start and end apart: 7, of which 7 were waited for; matrix products, arithmetic and copies ran while one was open for 1% of the time, Pallas kernels for 0%

commit v1 on v0

--- a/solution.py
+++ b/solution.py
@@ -4,6 +4,19 @@
 from jax.sharding import PartitionSpec as P
 
 SEQ_LEN = 128
+
+
+def collect_2(x, axis, dim):
+    ways = lax.axis_size(axis)
+    up = [(d, (d + 1) % ways) for d in range(ways)]
+    down = [(d, (d - 1) % ways) for d in range(ways)]
+    earlier, later = ([x], [x])
+    for _ in range(ways // 2):
+        earlier.append(lax.ppermute(earlier[-1], axis, up))
+    for _ in range((ways - 1) // 2):
+        later.append(lax.ppermute(later[-1], axis, down))
+    line = jnp.concatenate([*earlier[::-1], *later[1:]], axis=dim)
+    return jnp.roll(line, (lax.axis_index(axis) - ways // 2) * x.shape[dim], axis=dim)
 
 
 def partner(value, axis, bit):
@@ -99,7 +112,7 @@
     stored_rows = stored.shape[0]
     column = position * stored_rows + jnp.arange(stored_rows, dtype=jnp.int32)
     products = lax.dot_general(
-        lax.all_gather(queries, "row", axis=0, tiled=True),
+        collect_2(queries, "row", 0),
         stored,
         (((1,), (1,)), ((), ())),
         preferred_element_type=jnp.float32,

time: 382 us -> 407 us (1.065)
  starting transfers between devices: 14.5 us -> 45.4 us
  blocking collectives: 23 us -> 0 us
  waiting for transfers between devices: 254 us -> 270 us
    ppermute x0 -> x15, starting transfers between devices: none -> 31 us  [the longest x7 30.9 us: collect_2(): later.append(lax.ppermute(later[-1], axis, down))]
    all_gather x1 -> x0, blocking collectives: 23 us -> none  [shards(): lax.all_gather(queries, 'row', axis=0, tiled=True)]
    ppermute x0 -> x15, waiting for transfers between devices: none -> 15.9 us  [the longest x8 15.7 us: collect_2(): earlier.append(lax.ppermute(earlier[-1], axis, up))]
  transfers between devices with their start and end apart: 7 -> 22, of which waited for: 7 -> 15; matrix products, arithmetic and copies ran while one was open for 1% -> 1% of each run, Pallas kernels for 0% -> 0%
where the time goes in v1:
time: 407 us; the launch traced here: 406 us
  waiting for transfers between devices  270 us (66%)
  starting transfers between devices  45.4 us (11%)
  local copies, waits for them, and re-layouts  41.5 us (10%)
  other arithmetic  24.4 us (6%)
  matrix products  23.6 us (6%)
    ppermute x7, waiting for transfers between devices, partner(): lax.ppermute(value, axis, [(i, i ^ 1 << bit) for i in range(lax.axis_size...  254 us
    ppermute x7, starting transfers between devices, collect_2(): later.append(lax.ppermute(later[-1], axis, down))  30.9 us
    rev x7, local copies, waits for them, and re-layouts, xor_order(): flipped = shaped[:, ::-1].reshape(slot_data.shape)  18.3 us
    ppermute x8, waiting for transfers between devices, collect_2(): earlier.append(lax.ppermute(earlier[-1], axis, up))  15.7 us
    ppermute x7, starting transfers between devices, partner(): lax.ppermute(value, axis, [(i, i ^ 1 << bit) for i in range(lax.axis_size...  14.5 us
    dot_general x1, matrix products, shards(): lax.dot_general(grad_group, weights_lane, (((1,), (1,)), ((), ())), prefe...  14.3 us
    select_n x5, other arithmetic, xor_order(): slot_data = jnp.where(lane_id >> bit_level & 1 == 1, flipped, slot_data)  12.6 us
  transfers between devices with their start and end apart: 22, of which 15 were waited for; matrix products, arithmetic and copies ran while one was open for 1% of the time, Pallas kernels for 0%

profile of v1, /device:TPU:0, one launch (start us, length us, event | category | flops | bytes accessed | tf_op | source)
XLA Modules:
  0.0 405.8 jit_solution(17902511318726205276)
XLA Ops:
  0.0 0.5 collective-permute-start
  0.5 2.6 collective-permute-done
  3.1 3.3 maximum_select_fusion.5
  6.4 2.9 collective-permute-start.1
  9.3 46.0 %collective-permute-done.1 = bf16[256,4096]{1,0:T(8,128)(2,1)} collective-permute-done((bf16[256,4096]{1,0:T(8,128)(2,1)S(1)}, bf16[256,4096]{1,0:T(8,128)(2,1)}, u32[]{:S(2)}, u32[]{:S(2)}) %collective-permute-start.1) | collective-permute-done | bytes 2097184 | tf_op jit(solution)/shard_map/ppermute | solution.py:23
  55.3 4.7 %maximum_select_fusion.4 = bf16[512,4096]{1,0:T(8,128)(2,1)} fusion(bf16[256,4096]{1,0:T(8,128)(2,1)S(1)} %maximum_select_fusion.5, bf16[256,4096]{1,0:T(8,128)(2,1)} %collective-permute-done.1, pred[]{:T(512)S(6)} %eq.33), kind=kLoop, calls=%fused_computation.17 | loop fusion | flops 18874368 | bytes 8388609 | tf_op jit(solution)/shard_map/jit(_where)/select_n | solution.py:30
  60.0 1.8 collective-permute-start.2
  61.8 2.6 collective-permute-start.3
  64.4 165.7 %collective-permute-done.3 = bf16[448,4096]{1,0:T(8,128)(2,1)} collective-permute-done((bf16[448,4096]{1,0:T(8,128)(2,1)}, bf16[448,4096]{1,0:T(8,128)(2,1)}, u32[]{:S(2)}, u32[]{:S(2)}) %collective-permute-start.3) | collective-permute-done | bytes 3670048 | tf_op jit(solution)/shard_map/ppermute | solution.py:23
  230.1 1.0 collective-permute-done.2
  231.1 14.3 %fusion.20 = bf16[1024,896]{1,0:T(8,128)(2,1)S(1)} fusion(bf16[448,4096]{1,0:T(8,128)(2,1)} %param.11, bf16[448,4096]{1,0:T(8,128)(2,1)} %collective-permute-done.3, pred[]{:T(512)S(6)} %eq.35, bf16[512,4096]{1,0:T(8,128)(2,1)} %maximum_select_fusion.4, bf16[512,4096]{1,0:T(8,128)(2,1)} %collective-permute-done.2, pred[]{:T(512)S(6)} %eq.32), kind=kOutput, calls=%fused_computation.35 | convolution fusion | flops 7587889152 | bytes 17563650 | tf_op jit(solution)/shard_map/dot_general | solution.py:87
  245.4 1.4 rev.18
  246.8 3.6 copy.15
  250.4 2.4 copy.16
  252.8 2.9 broadcast_select_fusion
  255.7 2.9 rev.19
  258.6 2.4 copy.18
  261.0 3.0 select_select_fusion.2
  264.0 2.9 rev.20
  266.9 3.6 copy.20
  270.5 3.6 copy.19
  274.1 0.8 select_select_fusion.1
  274.9 1.1 fusion.36
  276.0 0.6 copy.21
  276.6 2.2 collective-permute-done.4
  278.8 1.6 copy.22
  280.4 0.2 fusion.28
  280.5 3.5 collective-permute-start.5
  284.1 20.7 %collective-permute-done.5 = bf16[2,2,128,896]{2,3,1,0:T(8,128)(2,1)S(1)} collective-permute-done((bf16[2,2,128,896]{2,3,1,0:T(8,128)(2,1)S(1)}, bf16[2,2,128,896]{2,3,1,0:T(8,128)(2,1)S(1)}, u32[]{:S(2)}, u32[]{:S(2)}) %collective-permute-start.5) | collective-permute-done | bytes 917536 | tf_op jit(solution)/shard_map/ppermute | solution.py:23
  304.7 0.2 pad_maximum_fusion
  304.9 1.1 fusion.35
  305.9 3.1 collective-permute-start.6
  309.1 3.9 copy.25
  313.0 0.4 convolution_convert_fusion
  313.4 16.0 %collective-permute-done.6 = bf16[1,4,128,896]{2,3,1,0:T(8,128)(2,1)S(1)} collective-permute-done((bf16[1,4,128,896]{2,3,1,0:T(8,128)(2,1)}, bf16[1,4,128,896]{2,3,1,0:T(8,128)(2,1)S(1)}, u32[]{:S(2)}, u32[]{:S(2)}) %collective-permute-start.6) | collective-permute-done | bytes 917536 | tf_op jit(solution)/shard_map/ppermute | solution.py:23
  329.4 1.6 pad_maximum_fusion.1
  331.1 1.6 rev.21
  332.7 2.9 maximum_select_fusion.6
  335.7 2.9 rev.22
  338.5 2.9 select_select_fusion
  341.5 3.0 rev.23
  344.4 1.8 select_bitcast_fusion
  346.3 1.3 copy.24
  347.6 0.8 copy-done.3
  348.4 3.7 multiply_reduce_fusion
  352.8 0.1 convert_element_type.41
  352.9 4.4 %collective-permute-start.15 = (bf16[1,4096]{1,0:T(2,128)(2,1)S(1)}, bf16[1,4096]{1,0:T(2,128)(2,1)S(1)}, u32[]{:S(2)}, u32[]{:S(2)}) collective-permute-start(bf16[1,4096]{1,0:T(2,128)(2,1)S(1)} %convert_element_type.41), channel_id=1, source_target_pairs={{0,15},{1,0},{2,1},{3,2},{4,3},{5,4},{6,5},{7,6},{8,7},{9,8},{10,9... | collective-permute-start | bytes 24584 | tf_op jit(solution)/shard_map/ppermute | solution.py:17
  357.4 1.4 collective-permute-done.7
  358.8 4.4 %collective-permute-start.16 = (bf16[1,4096]{1,0:T(2,128)(2,1)S(1)}, bf16[1,4096]{1,0:T(2,128)(2,1)S(1)}, u32[]{:S(2)}, u32[]{:S(2)}) collective-permute-start(bf16[1,4096]{1,0:T(2,128)(2,1)S(1)} %collective-permute-done.15), channel_id=1, source_target_pairs={{0,15},{1,0},{2,1},{3,2},{4,3},{5,4},{6,5},{7,6},{8,7},{9,8},{10,9... | collective-permute-start | bytes 24584 | tf_op jit(solution)/shard_map/ppermute | solution.py:17
  363.2 1.4 collective-permute-done.8
  364.7 0.0 collective-permute-done.16
  364.7 4.4 %collective-permute-start.17 = (bf16[1,4096]{1,0:T(2,128)(2,1)S(1)}, bf16[1,4096]{1,0:T(2,128)(2,1)S(1)}, u32[]{:S(2)}, u32[]{:S(2)}) collective-permute-start(bf16[1,4096]{1,0:T(2,128)(2,1)S(1)} %collective-permute-done.16), channel_id=1, source_target_pairs={{0,15},{1,0},{2,1},{3,2},{4,3},{5,4},{6,5},{7,6},{8,7},{9,8},{10,9... | collective-permute-start | bytes 24584 | tf_op jit(solution)/shard_map/ppermute | solution.py:17
  369.1 1.4 collective-permute-done.9
  370.6 4.4 %collective-permute-start.18 = (bf16[1,4096]{1,0:T(2,128)(2,1)S(1)}, bf16[1,4096]{1,0:T(2,128)(2,1)S(1)}, u32[]{:S(2)}, u32[]{:S(2)}) collective-permute-start(bf16[1,4096]{1,0:T(2,128)(2,1)S(1)} %collective-permute-done.17), channel_id=1, source_target_pairs={{0,15},{1,0},{2,1},{3,2},{4,3},{5,4},{6,5},{7,6},{8,7},{9,8},{10,9... | collective-permute-start | bytes 24584 | tf_op jit(solution)/shard_map/ppermute | solution.py:17
  375.0 1.4 collective-permute-done.10
  376.4 4.4 %collective-permute-start.19 = (bf16[1,4096]{1,0:T(2,128)(2,1)S(1)}, bf16[1,4096]{1,0:T(2,128)(2,1)S(1)}, u32[]{:S(2)}, u32[]{:S(2)}) collective-permute-start(bf16[1,4096]{1,0:T(2,128)(2,1)S(1)} %collective-permute-done.18), channel_id=1, source_target_pairs={{0,15},{1,0},{2,1},{3,2},{4,3},{5,4},{6,5},{7,6},{8,7},{9,8},{10,9... | collective-permute-start | bytes 24584 | tf_op jit(solution)/shard_map/ppermute | solution.py:17
  380.8 1.4 collective-permute-done.11
  382.3 4.4 %collective-permute-start.20 = (bf16[1,4096]{1,0:T(2,128)(2,1)S(1)}, bf16[1,4096]{1,0:T(2,128)(2,1)S(1)}, u32[]{:S(2)}, u32[]{:S(2)}) collective-permute-start(bf16[1,4096]{1,0:T(2,128)(2,1)S(1)} %collective-permute-done.19), channel_id=1, source_target_pairs={{0,15},{1,0},{2,1},{3,2},{4,3},{5,4},{6,5},{7,6},{8,7},{9,8},{10,9... | collective-permute-start | bytes 24584 | tf_op jit(solution)/shard_map/ppermute | solution.py:17
  386.7 1.4 collective-permute-done.12
  388.1 4.4 %collective-permute-start.21 = (bf16[1,4096]{1,0:T(2,128)(2,1)S(1)}, bf16[1,4096]{1,0:T(2,128)(2,1)S(1)}, u32[]{:S(2)}, u32[]{:S(2)}) collective-permute-start(bf16[1,4096]{1,0:T(2,128)(2,1)S(1)} %collective-permute-done.20), channel_id=1, source_target_pairs={{0,15},{1,0},{2,1},{3,2},{4,3},{5,4},{6,5},{7,6},{8,7},{9,8},{10,9... | collective-permute-start | bytes 24584 | tf_op jit(solution)/shard_map/ppermute | solution.py:17
  392.6 1.4 collective-permute-done.13
  394.0 5.8 %collective-permute-done.14 = bf16[1,4096]{1,0:T(2,128)(2,1)S(1)} collective-permute-done((bf16[1,4096]{1,0:T(2,128)(2,1)S(1)}, bf16[1,4096]{1,0:T(2,128)(2,1)S(1)}, u32[]{:S(2)}, u32[]{:S(2)}) %collective-permute-start.14) | collective-permute-done | bytes 8224 | tf_op jit(solution)/shard_map/ppermute | solution.py:15
  399.8 0.8 concatenate.73
  400.6 5.1 %convolution_select_fusion = f32[16,768]{1,0:T(8,128)} fusion(bf16[768,4096]{1,0:T(8,128)(2,1)} %param.14, bf16[32,4096]{1,0:T(8,128)(2,1)S(1)} %concatenate.73, s32[]{:T(128)S(6)} %select_n.178, s32[768]{0:T(1024)S(1)} %iota_add_fusion, s32[16]{0:T(128)S(1)} %copy-done.5), kind=kOutput, calls=%fused_computation.37 | convolution fusion | flops 100687872 | bytes 6476292 | tf_op jit(solution)/shard_map/dot_general | solution.py:114
  (28 shorter events, 0.2 us)
Async XLA Ops:
  0.0 313.0 %copy-start = (bf16[128,4096]{1,0:T(8,128)(2,1)S(1)}, bf16[128,4096]{1,0:T(8,128)(2,1)}, u32[]{:S(2)}) copy-start(bf16[128,4096]{1,0:T(8,128)(2,1)} %param.8) | copy-start | bytes 3145732
  0.0 3.1 collective-permute-start
  6.4 49.0 %collective-permute-start.1 = (bf16[256,4096]{1,0:T(8,128)(2,1)S(1)}, bf16[256,4096]{1,0:T(8,128)(2,1)}, u32[]{:S(2)}, u32[]{:S(2)}) collective-permute-start(bf16[256,4096]{1,0:T(8,128)(2,1)S(1)} %maximum_select_fusion.5), channel_id=1, source_target_pairs={{0,2},{1,3},{2,0},{3,1},{4,6},{5,7},{6,4},{7,5},{8,10},{9,11},{10,... | collective-permute-start | bytes 6291464 | tf_op jit(solution)/shard_map/ppermute | solution.py:23
  60.0 171.1 %collective-permute-start.2 = (bf16[512,4096]{1,0:T(8,128)(2,1)}, bf16[512,4096]{1,0:T(8,128)(2,1)}, u32[]{:S(2)}, u32[]{:S(2)}) collective-permute-start(bf16[512,4096]{1,0:T(8,128)(2,1)} %maximum_select_fusion.4), channel_id=1, source_target_pairs={{0,4},{1,5},{2,6},{3,7},{4,0},{5,1},{6,2},{7,3},{8,12},{9,13},{10,... | collective-permute-start | bytes 12582920 | tf_op jit(solution)/shard_map/ppermute | solution.py:23
  61.8 168.3 %collective-permute-start.3 = (bf16[448,4096]{1,0:T(8,128)(2,1)}, bf16[448,4096]{1,0:T(8,128)(2,1)}, u32[]{:S(2)}, u32[]{:S(2)}) collective-permute-start(bf16[448,4096]{1,0:T(8,128)(2,1)} %param.11), channel_id=1, source_target_pairs={{0,8},{1,9},{2,10},{3,11},{4,12},{5,13},{6,14},{7,15},{8,0},{9,1},... | collective-permute-start | bytes 11010056 | tf_op jit(solution)/shard_map/ppermute | solution.py:23
  276.0 2.8 collective-permute-start.4
  280.5 24.2 %collective-permute-start.5 = (bf16[2,2,128,896]{2,3,1,0:T(8,128)(2,1)S(1)}, bf16[2,2,128,896]{2,3,1,0:T(8,128)(2,1)S(1)}, u32[]{:S(2)}, u32[]{:S(2)}) collective-permute-start(bf16[2,2,128,896]{2,3,1,0:T(8,128)(2,1)S(1)} %get-tuple-element.8), channel_id=1, source_target_pairs={{0,2},{1,3},{2,0},{3,1},{4,6},{5,7},{6,4},{7,5},{8,10},{9,11},{10,... | collective-permute-start | bytes 2752520 | tf_op jit(solution)/shard_map/ppermute | solution.py:23
  305.9 23.5 %copy-start.1 = (bf16[1,1,4,128,896]{3,4,2,1,0:T(8,128)(2,1)}, bf16[1,1,4,128,896]{3,4,2,1,0:T(8,128)(2,1)S(1)}, u32[]{:S(2)}) copy-start(bf16[1,1,4,128,896]{3,4,2,1,0:T(8,128)(2,1)S(1)} %get-tuple-element.5) | copy-start | bytes 2752516
  305.9 7.0 %copy-start.4 = (bf16[4096,64]{0,1:T(8,128)(2,1)S(1)}, bf16[4096,64]{0,1:T(8,128)(2,1)}, u32[]{:S(2)}) copy-start(bf16[4096,64]{0,1:T(8,128)(2,1)} %param.12) | copy-start | bytes 1572868
  305.9 23.5 %collective-permute-start.6 = (bf16[1,4,128,896]{2,3,1,0:T(8,128)(2,1)}, bf16[1,4,128,896]{2,3,1,0:T(8,128)(2,1)S(1)}, u32[]{:S(2)}, u32[]{:S(2)}) collective-permute-start(bf16[1,4,128,896]{2,3,1,0:T(8,128)(2,1)} %get-tuple-element.6), channel_id=1, source_target_pairs={{0,4},{1,5},{2,6},{3,7},{4,0},{5,1},{6,2},{7,3},{8,12},{9,13},{10,... | collective-permute-start | bytes 2752520 | tf_op jit(solution)/shard_map/ppermute | solution.py:23
  329.4 1.6 copy-start.2
  346.3 2.2 copy-start.3
  348.4 52.2 %copy-start.5 = (s32[16]{0:T(128)S(1)}, s32[16]{0:T(128)}, u32[]{:S(2)}) copy-start(s32[16]{0:T(128)} %param.15) | copy-start | bytes 196
  352.9 5.9 %collective-permute-start.7 = (bf16[1,4096]{1,0:T(2,128)(2,1)S(1)}, bf16[1,4096]{1,0:T(2,128)(2,1)S(1)}, u32[]{:S(2)}, u32[]{:S(2)}) collective-permute-start(bf16[1,4096]{1,0:T(2,128)(2,1)S(1)} %convert_element_type.41), channel_id=1, source_target_pairs={{0,1},{1,2},{2,3},{3,4},{4,5},{5,6},{6,7},{7,8},{8,9},{9,10},{10,1... | collective-permute-start | bytes 24584 | tf_op jit(solution)/shard_map/ppermute | solution.py:15
  352.9 5.9 %collective-permute-start.15 = (bf16[1,4096]{1,0:T(2,128)(2,1)S(1)}, bf16[1,4096]{1,0:T(2,128)(2,1)S(1)}, u32[]{:S(2)}, u32[]{:S(2)}) collective-permute-start(bf16[1,4096]{1,0:T(2,128)(2,1)S(1)} %convert_element_type.41), channel_id=1, source_target_pairs={{0,15},{1,0},{2,1},{3,2},{4,3},{5,4},{6,5},{7,6},{8,7},{9,8},{10,9... | collective-permute-start | bytes 24584 | tf_op jit(solution)/shard_map/ppermute | solution.py:17
  358.8 5.9 %collective-permute-start.8 = (bf16[1,4096]{1,0:T(2,128)(2,1)S(1)}, bf16[1,4096]{1,0:T(2,128)(2,1)S(1)}, u32[]{:S(2)}, u32[]{:S(2)}) collective-permute-start(bf16[1,4096]{1,0:T(2,128)(2,1)S(1)} %collective-permute-done.7), channel_id=1, source_target_pairs={{0,1},{1,2},{2,3},{3,4},{4,5},{5,6},{6,7},{7,8},{8,9},{9,10},{10,1... | collective-permute-start | bytes 24584 | tf_op jit(solution)/shard_map/ppermute | solution.py:15
  358.8 5.9 %collective-permute-start.16 = (bf16[1,4096]{1,0:T(2,128)(2,1)S(1)}, bf16[1,4096]{1,0:T(2,128)(2,1)S(1)}, u32[]{:S(2)}, u32[]{:S(2)}) collective-permute-start(bf16[1,4096]{1,0:T(2,128)(2,1)S(1)} %collective-permute-done.15), channel_id=1, source_target_pairs={{0,15},{1,0},{2,1},{3,2},{4,3},{5,4},{6,5},{7,6},{8,7},{9,8},{10,9... | collective-permute-start | bytes 24584 | tf_op jit(solution)/shard_map/ppermute | solution.py:17
  364.7 5.9 %collective-permute-start.9 = (bf16[1,4096]{1,0:T(2,128)(2,1)S(1)}, bf16[1,4096]{1,0:T(2,128)(2,1)S(1)}, u32[]{:S(2)}, u32[]{:S(2)}) collective-permute-start(bf16[1,4096]{1,0:T(2,128)(2,1)S(1)} %collective-permute-done.8), channel_id=1, source_target_pairs={{0,1},{1,2},{2,3},{3,4},{4,5},{5,6},{6,7},{7,8},{8,9},{9,10},{10,1... | collective-permute-start | bytes 24584 | tf_op jit(solution)/shard_map/ppermute | solution.py:15
  364.7 5.9 %collective-permute-start.17 = (bf16[1,4096]{1,0:T(2,128)(2,1)S(1)}, bf16[1,4096]{1,0:T(2,128)(2,1)S(1)}, u32[]{:S(2)}, u32[]{:S(2)}) collective-permute-start(bf16[1,4096]{1,0:T(2,128)(2,1)S(1)} %collective-permute-done.16), channel_id=1, source_target_pairs={{0,15},{1,0},{2,1},{3,2},{4,3},{5,4},{6,5},{7,6},{8,7},{9,8},{10,9... | collective-permute-start | bytes 24584 | tf_op jit(solution)/shard_map/ppermute | solution.py:17
  370.5 5.9 %collective-permute-start.10 = (bf16[1,4096]{1,0:T(2,128)(2,1)S(1)}, bf16[1,4096]{1,0:T(2,128)(2,1)S(1)}, u32[]{:S(2)}, u32[]{:S(2)}) collective-permute-start(bf16[1,4096]{1,0:T(2,128)(2,1)S(1)} %collective-permute-done.9), channel_id=1, source_target_pairs={{0,1},{1,2},{2,3},{3,4},{4,5},{5,6},{6,7},{7,8},{8,9},{9,10},{10,1... | collective-permute-start | bytes 24584 | tf_op jit(solution)/shard_map/ppermute | solution.py:15
  370.6 5.9 %collective-permute-start.18 = (bf16[1,4096]{1,0:T(2,128)(2,1)S(1)}, bf16[1,4096]{1,0:T(2,128)(2,1)S(1)}, u32[]{:S(2)}, u32[]{:S(2)}) collective-permute-start(bf16[1,4096]{1,0:T(2,128)(2,1)S(1)} %collective-permute-done.17), channel_id=1, source_target_pairs={{0,15},{1,0},{2,1},{3,2},{4,3},{5,4},{6,5},{7,6},{8,7},{9,8},{10,9... | collective-permute-start | bytes 24584 | tf_op jit(solution)/shard_map/ppermute | solution.py:17
  376.4 5.9 %collective-permute-start.11 = (bf16[1,4096]{1,0:T(2,128)(2,1)S(1)}, bf16[1,4096]{1,0:T(2,128)(2,1)S(1)}, u32[]{:S(2)}, u32[]{:S(2)}) collective-permute-start(bf16[1,4096]{1,0:T(2,128)(2,1)S(1)} %collective-permute-done.10), channel_id=1, source_target_pairs={{0,1},{1,2},{2,3},{3,4},{4,5},{5,6},{6,7},{7,8},{8,9},{9,10},{10,1... | collective-permute-start | bytes 24584 | tf_op jit(solution)/shard_map/ppermute | solution.py:15
  376.4 5.9 %collective-permute-start.19 = (bf16[1,4096]{1,0:T(2,128)(2,1)S(1)}, bf16[1,4096]{1,0:T(2,128)(2,1)S(1)}, u32[]{:S(2)}, u32[]{:S(2)}) collective-permute-start(bf16[1,4096]{1,0:T(2,128)(2,1)S(1)} %collective-permute-done.18), channel_id=1, source_target_pairs={{0,15},{1,0},{2,1},{3,2},{4,3},{5,4},{6,5},{7,6},{8,7},{9,8},{10,9... | collective-permute-start | bytes 24584 | tf_op jit(solution)/shard_map/ppermute | solution.py:17
  382.2 5.9 %collective-permute-start.12 = (bf16[1,4096]{1,0:T(2,128)(2,1)S(1)}, bf16[1,4096]{1,0:T(2,128)(2,1)S(1)}, u32[]{:S(2)}, u32[]{:S(2)}) collective-permute-start(bf16[1,4096]{1,0:T(2,128)(2,1)S(1)} %collective-permute-done.11), channel_id=1, source_target_pairs={{0,1},{1,2},{2,3},{3,4},{4,5},{5,6},{6,7},{7,8},{8,9},{9,10},{10,1... | collective-permute-start | bytes 24584 | tf_op jit(solution)/shard_map/ppermute | solution.py:15
  382.3 5.9 %collective-permute-start.20 = (bf16[1,4096]{1,0:T(2,128)(2,1)S(1)}, bf16[1,4096]{1,0:T(2,128)(2,1)S(1)}, u32[]{:S(2)}, u32[]{:S(2)}) collective-permute-start(bf16[1,4096]{1,0:T(2,128)(2,1)S(1)} %collective-permute-done.19), channel_id=1, source_target_pairs={{0,15},{1,0},{2,1},{3,2},{4,3},{5,4},{6,5},{7,6},{8,7},{9,8},{10,9... | collective-permute-start | bytes 24584 | tf_op jit(solution)/shard_map/ppermute | solution.py:17
  388.1 5.9 %collective-permute-start.13 = (bf16[1,4096]{1,0:T(2,128)(2,1)S(1)}, bf16[1,4096]{1,0:T(2,128)(2,1)S(1)}, u32[]{:S(2)}, u32[]{:S(2)}) collective-permute-start(bf16[1,4096]{1,0:T(2,128)(2,1)S(1)} %collective-permute-done.12), channel_id=1, source_target_pairs={{0,1},{1,2},{2,3},{3,4},{4,5},{5,6},{6,7},{7,8},{8,9},{9,10},{10,1... | collective-permute-start | bytes 24584 | tf_op jit(solution)/shard_map/ppermute | solution.py:15
  388.1 5.9 %collective-permute-start.21 = (bf16[1,4096]{1,0:T(2,128)(2,1)S(1)}, bf16[1,4096]{1,0:T(2,128)(2,1)S(1)}, u32[]{:S(2)}, u32[]{:S(2)}) collective-permute-start(bf16[1,4096]{1,0:T(2,128)(2,1)S(1)} %collective-permute-done.20), channel_id=1, source_target_pairs={{0,15},{1,0},{2,1},{3,2},{4,3},{5,4},{6,5},{7,6},{8,7},{9,8},{10,9... | collective-permute-start | bytes 24584 | tf_op jit(solution)/shard_map/ppermute | solution.py:17
  394.0 5.9 %collective-permute-start.14 = (bf16[1,4096]{1,0:T(2,128)(2,1)S(1)}, bf16[1,4096]{1,0:T(2,128)(2,1)S(1)}, u32[]{:S(2)}, u32[]{:S(2)}) collective-permute-start(bf16[1,4096]{1,0:T(2,128)(2,1)S(1)} %collective-permute-done.13), channel_id=1, source_target_pairs={{0,1},{1,2},{2,3},{3,4},{4,5},{5,6},{6,7},{7,8},{8,9},{9,10},{10,1... | collective-permute-start | bytes 24584 | tf_op jit(solution)/shard_map/ppermute | solution.py:15
